TPU v7x, 32 devices: a whole 2x2x4 slice. The times are simulated.
32 devices in a mesh: fsdp: 16 (over z, y, core), expert: 2 (over x).
Axes of the slice: x: 2, y: 2, z: 4, core: 2. Of those that a mesh axis runs over, the one named last changes fastest.
Arguments:
- tokens: bfloat16 [8192, 1024], P(('fsdp', 'expert')), may hold values from -6 to 6
- query_weight: bfloat16 [1024, 1024], P(('fsdp', 'expert')), may hold values from -0.1875 to 0.1875
- key_projection: bfloat16 [1024, 512], P(('fsdp', 'expert')), may hold values from -0.1875 to 0.1875
- value_projection: bfloat16 [1024, 512], P(('fsdp', 'expert')), may hold values from -0.1875 to 0.1875
- output_weight: bfloat16 [1024, 1024], P(('fsdp', 'expert')), may hold values from -0.75 to 0.75
- router_weight: bfloat16 [1024, 32], P(('fsdp', 'expert')), may hold values from -0.375 to 0.375
- attn_gain: bfloat16 [1024], P(('fsdp', 'expert')), may hold values from 0.5 to 1.5
- ffn_gain: bfloat16 [1024], P(('fsdp', 'expert')), may hold values from 0.5 to 1.5
- gate_weight: bfloat16 [32, 1024, 512], P('expert', 'fsdp'), may hold values from -0.1875 to 0.1875
- up_weight: bfloat16 [32, 1024, 512], P('expert', 'fsdp'), may hold values from -0.1875 to 0.1875
- down_weight: bfloat16 [32, 512, 1024], P('expert', 'fsdp'), may hold values from -0.75 to 0.75
- lengths: int32 [32, 2, 4], P(('fsdp', 'expert')), may hold values from 1 to 64, 128 in all within a row
- routes: int32 [8192, 8], P(('fsdp', 'expert')), may hold values from 0 to 31, all different within a row; in each aligned block of 128 rows (0 to 127, 128 to 255, ...) at most 40 rows name the same one
- cotangent: bfloat16 [8192, 1024], P(('fsdp', 'expert')), may hold values from -6 to 6
Outputs:
- layer_out: bfloat16 [8192, 1024], P(('fsdp', 'expert'))
- grad_tokens: float32 [8192, 1024], P(('fsdp', 'expert'))
- grad_query: float32 [1024, 1024], P(('fsdp', 'expert'))
- grad_key: float32 [1024, 512], P(('fsdp', 'expert'))
- grad_value: float32 [1024, 512], P(('fsdp', 'expert'))
- grad_output: float32 [1024, 1024], P(('fsdp', 'expert'))
- grad_router: float32 [1024, 32], P(('fsdp', 'expert'))
- grad_attn_gain: float32 [1024], P(('fsdp', 'expert'))
- grad_ffn_gain: float32 [1024], P(('fsdp', 'expert'))
- grad_gate: float32 [32, 1024, 512], P('expert', 'fsdp')
- grad_up: float32 [32, 1024, 512], P('expert', 'fsdp')
- grad_down: float32 [32, 512, 1024], P('expert', 'fsdp')
Inputs may be any that keep to these rules, and one draw needn't show every extreme that they name: Each micro-batch of each device holds 4 sequences whose lengths sum to 128; the longest is exactly 64 tokens in every micro-batch. `routes`: the 8 experts of a row differ; in each aligned block of 128 rows (one micro-batch of one device) no expert is named by more than 40 rows, a bound that some block reaches.
All inputs are finite; a program needn't handle non-finite values.
Results may differ from a plain program's by a relative error of at most 0.015.
The roundings to bfloat16 on the way count: a program that leaves them out, or rounds other values in their place, can miss the bound.
Values may be sent and summed in bfloat16 or wider, within the bound.
No kernel may reach another device: no remote copies, remote signals or barrier semaphores. Data moves between devices by JAX's collectives and lax.ppermute only.
A program may use at most 256 MiB of HBM per device.

v0:
```python
import jax
import jax.numpy as jnp
from jax import lax
from jax.sharding import PartitionSpec as P

MODEL_WIDTH = 1024
QUERY_HEADS = 16
KEY_VALUE_HEADS = 8
HEAD_SIZE = 64
EXPERTS = 32
TOPK = 8
DEVICE_TOKENS = 128
MB = 2
CAP = 40


EPS = 1e-06
THETA = 10000.0
SCALE = 0.125
HIGH = lax.Precision.HIGHEST


def as_sent(x):
    return jax.tree.map(lambda a: a.astype(jnp.bfloat16) if a.dtype == jnp.float32 else a, x)


def sequence_layout(seq_lengths, row_number):
    row_index = jnp.arange(row_number, dtype=jnp.int32)
    seq_ends = jnp.cumsum(seq_lengths)
    starts = seq_ends - seq_lengths
    member = (
        (row_index[:, None] >= starts[None, :]) & (row_index[:, None] < seq_ends[None, :])
    ).astype(jnp.int32)
    labels = jnp.arange(seq_lengths.shape[0], dtype=jnp.int32)
    segment = jnp.sum(member * labels[None, :], axis=1)
    offset = jnp.sum(member * starts[None, :], axis=1)
    return (segment, row_index - offset)


def rotary_apply(values, token_positions, reverse):
    half_width = values.shape[-1] // 2
    frequency = THETA ** (-2.0 * jnp.arange(half_width, dtype=jnp.float32) / values.shape[-1])
    angles = token_positions.astype(jnp.float32)[:, None] * frequency[None, :]
    cosine = jnp.cos(angles)[:, None, :]
    sine_part = jnp.sin(angles)[:, None, :]
    if reverse:
        sine_part = -sine_part
    first_half = values[..., :half_width]
    second_half = values[..., half_width:]
    return jnp.concatenate(
        [
            first_half * cosine - second_half * sine_part,
            second_half * cosine + first_half * sine_part,
        ],
        axis=-1,
    )


def rms_scale(values):
    return lax.rsqrt(jnp.mean(values * values, axis=1, keepdims=True) + EPS)


def norm_back(grad_normed, gain_vec, plain_part, scale_part):
    grad_gain = jnp.sum(grad_normed * plain_part, axis=0)
    shaped = grad_normed * gain_vec[None, :]
    grad_input = scale_part * (
        shaped - plain_part * jnp.mean(shaped * plain_part, axis=1, keepdims=True)
    )
    return (grad_input, grad_gain)


def fetch_dense(
    query_weight,
    key_projection,
    value_projection,
    output_weight,
    router_weight,
    attn_gain,
    ffn_gain,
):
    return (
        lax.all_gather(query_weight, ("fsdp", "expert"), axis=0, tiled=True),
        lax.all_gather(key_projection, ("fsdp", "expert"), axis=0, tiled=True),
        lax.all_gather(value_projection, ("fsdp", "expert"), axis=0, tiled=True),
        lax.all_gather(output_weight, ("fsdp", "expert"), axis=0, tiled=True),
        lax.all_gather(router_weight, ("fsdp", "expert"), axis=0, tiled=True),
        lax.all_gather(attn_gain, ("fsdp", "expert"), axis=0, tiled=True),
        lax.all_gather(ffn_gain, ("fsdp", "expert"), axis=0, tiled=True),
    )


def fetch_experts(gate_weight, up_weight, down_weight):
    return (
        lax.all_gather(gate_weight, "fsdp", axis=1, tiled=True),
        lax.all_gather(up_weight, "fsdp", axis=1, tiled=True),
        lax.all_gather(down_weight, "fsdp", axis=1, tiled=True),
    )


def per_device(
    tokens,
    query_weight,
    key_projection,
    value_projection,
    output_weight,
    router_weight,
    attn_gain,
    ffn_gain,
    gate_weight,
    up_weight,
    down_weight,
    lengths,
    routes,
    cotangent,
):
    groups = lax.axis_size("expert")
    local_experts = gate_weight.shape[0]
    query_group_width = QUERY_HEADS // KEY_VALUE_HEADS
    outputs = []
    input_grads = []
    sums_dense = None
    sums_expert = None
    for batch_index in range(MB):
        dense_set = fetch_dense(
            query_weight,
            key_projection,
            value_projection,
            output_weight,
            router_weight,
            attn_gain,
            ffn_gain,
        )
        expert_set = fetch_experts(gate_weight, up_weight, down_weight)
        q_full, key_expanded, v_full, o_full, r_full, gain_one, gain_two = dense_set
        gate_full, up_full, down_full = expert_set
        row_start = batch_index * DEVICE_TOKENS
        plain_in = tokens[row_start : row_start + DEVICE_TOKENS].astype(jnp.float32)
        grad_out = cotangent[row_start : row_start + DEVICE_TOKENS].astype(jnp.float32)
        segment, token_positions = sequence_layout(lengths[0, batch_index], DEVICE_TOKENS)
        row_index = jnp.arange(DEVICE_TOKENS, dtype=jnp.int32)
        allowed = (segment[:, None] == segment[None, :]) & (
            row_index[:, None] >= row_index[None, :]
        )
        scale_one = rms_scale(plain_in)
        plain_one = plain_in * scale_one
        attention_input = (plain_one * gain_one.astype(jnp.float32)[None, :]).astype(jnp.bfloat16)
        query_rows = rotary_apply(
            jnp.dot(attention_input, q_full, preferred_element_type=jnp.float32).reshape(
                DEVICE_TOKENS, QUERY_HEADS, HEAD_SIZE
            ),
            token_positions,
            False,
        ).astype(jnp.bfloat16)
        key_matrix_rows = rotary_apply(
            jnp.dot(attention_input, key_expanded, preferred_element_type=jnp.float32).reshape(
                DEVICE_TOKENS, KEY_VALUE_HEADS, HEAD_SIZE
            ),
            token_positions,
            False,
        ).astype(jnp.bfloat16)
        value_matrix_rows = (
            jnp.dot(attention_input, v_full, preferred_element_type=jnp.float32)
            .astype(jnp.bfloat16)
            .reshape(DEVICE_TOKENS, KEY_VALUE_HEADS, HEAD_SIZE)
        )
        query_grouped = query_rows.reshape(
            DEVICE_TOKENS, KEY_VALUE_HEADS, query_group_width, HEAD_SIZE
        )
        scores = (
            jnp.einsum(
                "qgrd,kgd->grqk", query_grouped, key_matrix_rows, preferred_element_type=jnp.float32
            )
            * SCALE
        )
        scores = jnp.where(allowed, scores, -1e30)
        row_max = jnp.max(scores, axis=-1, keepdims=True)
        exp_scores = jnp.exp(scores - row_max)
        row_total = jnp.sum(exp_scores, axis=-1, keepdims=True)
        attn_probs = exp_scores / row_total
        log_total = row_max + jnp.log(row_total)
        attention_mixed = (
            jnp.einsum(
                "grqk,kgd->qgrd",
                attn_probs.astype(jnp.bfloat16),
                value_matrix_rows,
                preferred_element_type=jnp.float32,
            )
            .reshape(DEVICE_TOKENS, QUERY_HEADS * HEAD_SIZE)
            .astype(jnp.bfloat16)
        )
        middle = plain_in + jnp.dot(attention_mixed, o_full, preferred_element_type=jnp.float32)
        scale_two = rms_scale(middle)
        plain_two = middle * scale_two
        ffn_in = (plain_two * gain_two.astype(jnp.float32)[None, :]).astype(jnp.bfloat16)
        logits = jnp.dot(ffn_in, r_full, preferred_element_type=jnp.float32)
        picked = routes[row_start : row_start + DEVICE_TOKENS]
        chosen = picked[:, :, None] == jnp.arange(EXPERTS, dtype=jnp.int32)[None, None, :]
        chosen_float = chosen.astype(jnp.float32)
        gate_probs = jax.nn.softmax(jnp.sum(logits[:, None, :] * chosen_float, axis=2), axis=1)
        expert_hits = jnp.sum(chosen.astype(jnp.int32), axis=1)
        before = jnp.cumsum(expert_hits, axis=0) - expert_hits
        slot_rank = jnp.sum(jnp.where(chosen, before[:, None, :], 0), axis=2)
        slot_of = (picked * CAP + slot_rank).reshape(-1)
        slot_table = (
            jnp.full((EXPERTS * CAP,), DEVICE_TOKENS * TOPK, jnp.int32)
            .at[slot_of]
            .set(jnp.arange(DEVICE_TOKENS * TOPK, dtype=jnp.int32))
        )
        padded_in = jnp.concatenate([ffn_in, jnp.zeros((1, MODEL_WIDTH), jnp.bfloat16)], axis=0)
        dispatch_rows = jnp.take(padded_in, slot_table // TOPK, axis=0).reshape(
            groups, local_experts, CAP, MODEL_WIDTH
        )
        received = lax.all_to_all(dispatch_rows, "expert", split_axis=0, concat_axis=0, tiled=True)
        gate_act = jnp.einsum(
            "sltd,ldh->slth", received, gate_full, preferred_element_type=jnp.float32
        )
        up_act = jnp.einsum("sltd,ldh->slth", received, up_full, preferred_element_type=jnp.float32)
        sigmoid_g = jax.nn.sigmoid(gate_act)
        silu_gate = gate_act * sigmoid_g
        hidden = (silu_gate * up_act).astype(jnp.bfloat16)
        produced = jnp.einsum(
            "slth,lhd->sltd", hidden, down_full, preferred_element_type=jnp.float32
        ).astype(jnp.bfloat16)
        returned = lax.all_to_all(
            produced, "expert", split_axis=0, concat_axis=0, tiled=True
        ).reshape(EXPERTS * CAP, MODEL_WIDTH)
        picked_rows = (
            jnp.take(returned, slot_of, axis=0)
            .reshape(DEVICE_TOKENS, TOPK, MODEL_WIDTH)
            .astype(jnp.float32)
        )
        combined = jnp.sum(gate_probs[:, :, None] * picked_rows, axis=1)
        outputs.append((middle + combined).astype(jnp.bfloat16))
        dense_set = fetch_dense(
            query_weight,
            key_projection,
            value_projection,
            output_weight,
            router_weight,
            attn_gain,
            ffn_gain,
        )
        expert_set = fetch_experts(gate_weight, up_weight, down_weight)
        q_full, key_expanded, v_full, o_full, r_full, gain_one, gain_two = dense_set
        gate_full, up_full, down_full = expert_set
        grad_gate = jnp.sum(grad_out[:, None, :] * picked_rows, axis=2)
        grad_choice = gate_probs * (
            grad_gate - jnp.sum(gate_probs * grad_gate, axis=1, keepdims=True)
        )
        grad_logits = jnp.sum(grad_choice[:, :, None] * chosen_float, axis=1)
        grad_router = jnp.dot(ffn_in.astype(jnp.float32).T, grad_logits, precision=HIGH)
        grad_ffn_in = jnp.dot(grad_logits, r_full.astype(jnp.float32).T, precision=HIGH)
        grad_produced = (
            (gate_probs[:, :, None] * grad_out[:, None, :])
            .astype(jnp.bfloat16)
            .reshape(DEVICE_TOKENS * TOPK, MODEL_WIDTH)
        )
        padded_grad = jnp.concatenate(
            [grad_produced, jnp.zeros((1, MODEL_WIDTH), jnp.bfloat16)], axis=0
        )
        grad_dispatch = jnp.take(padded_grad, slot_table, axis=0).reshape(
            groups, local_experts, CAP, MODEL_WIDTH
        )
        grad_recv = lax.all_to_all(grad_dispatch, "expert", split_axis=0, concat_axis=0, tiled=True)
        grad_hidden = jnp.einsum(
            "sltd,lhd->slth", grad_recv, down_full, preferred_element_type=jnp.float32
        )
        grad_down_w = jnp.einsum(
            "slth,sltd->lhd", hidden, grad_recv, preferred_element_type=jnp.float32
        )
        grad_gact = (
            grad_hidden * up_act * sigmoid_g * (1.0 + gate_act * (1.0 - sigmoid_g))
        ).astype(jnp.bfloat16)
        grad_uact = (grad_hidden * silu_gate).astype(jnp.bfloat16)
        grad_gate_w = jnp.einsum(
            "sltd,slth->ldh", received, grad_gact, preferred_element_type=jnp.float32
        )
        grad_up_w = jnp.einsum(
            "sltd,slth->ldh", received, grad_uact, preferred_element_type=jnp.float32
        )
        grad_inputs = (
            jnp.einsum("slth,ldh->sltd", grad_gact, gate_full, preferred_element_type=jnp.float32)
            + jnp.einsum("slth,ldh->sltd", grad_uact, up_full, preferred_element_type=jnp.float32)
        ).astype(jnp.bfloat16)
        grad_back = lax.all_to_all(
            grad_inputs, "expert", split_axis=0, concat_axis=0, tiled=True
        ).reshape(EXPERTS * CAP, MODEL_WIDTH)
        grad_ffn_in = grad_ffn_in + jnp.sum(
            jnp.take(grad_back, slot_of, axis=0)
            .reshape(DEVICE_TOKENS, TOPK, MODEL_WIDTH)
            .astype(jnp.float32),
            axis=1,
        )
        grad_middle, grad_gain_two = norm_back(
            grad_ffn_in, gain_two.astype(jnp.float32), plain_two, scale_two
        )
        grad_middle = grad_middle + grad_out
        grad_attn = grad_middle.astype(jnp.bfloat16)
        grad_out_w = jnp.einsum(
            "te,td->ed", attention_mixed, grad_attn, preferred_element_type=jnp.float32
        )
        grad_mix = (
            jnp.einsum("td,ed->te", grad_attn, o_full, preferred_element_type=jnp.float32)
            .astype(jnp.bfloat16)
            .reshape(DEVICE_TOKENS, KEY_VALUE_HEADS, query_group_width, HEAD_SIZE)
        )
        scores_again = (
            jnp.einsum(
                "qgrd,kgd->grqk", query_grouped, key_matrix_rows, preferred_element_type=jnp.float32
            )
            * SCALE
        )
        scores_again = jnp.where(allowed, scores_again, -1e30)
        probs_again = jnp.exp(scores_again - log_total)
        grad_value = (
            jnp.einsum(
                "grqk,qgrd->kgd",
                probs_again.astype(jnp.bfloat16),
                grad_mix,
                preferred_element_type=jnp.float32,
            )
            .astype(jnp.bfloat16)
            .reshape(DEVICE_TOKENS, KEY_VALUE_HEADS * HEAD_SIZE)
        )
        grad_probs = jnp.einsum(
            "qgrd,kgd->grqk", grad_mix, value_matrix_rows, preferred_element_type=jnp.float32
        )
        row_inner = jnp.sum(probs_again * grad_probs, axis=-1, keepdims=True)
        grad_scores = (probs_again * (grad_probs - row_inner)).astype(jnp.bfloat16)
        grad_queries = (
            jnp.einsum(
                "grqk,kgd->qgrd", grad_scores, key_matrix_rows, preferred_element_type=jnp.float32
            )
            * SCALE
        )
        grad_queries = (
            rotary_apply(
                grad_queries.reshape(DEVICE_TOKENS, QUERY_HEADS, HEAD_SIZE), token_positions, True
            )
            .astype(jnp.bfloat16)
            .reshape(DEVICE_TOKENS, QUERY_HEADS * HEAD_SIZE)
        )
        key_gradients = (
            jnp.einsum(
                "grqk,qgrd->kgd", grad_scores, query_grouped, preferred_element_type=jnp.float32
            )
            * SCALE
        )
        key_gradients = (
            rotary_apply(key_gradients, token_positions, True)
            .astype(jnp.bfloat16)
            .reshape(DEVICE_TOKENS, KEY_VALUE_HEADS * HEAD_SIZE)
        )
        grad_query_w = jnp.einsum(
            "td,te->de", attention_input, grad_queries, preferred_element_type=jnp.float32
        )
        grad_key_w = jnp.einsum(
            "td,te->de", attention_input, key_gradients, preferred_element_type=jnp.float32
        )
        grad_value_w = jnp.einsum(
            "td,te->de", attention_input, grad_value, preferred_element_type=jnp.float32
        )
        grad_attn_in = jnp.einsum(
            "te,de->td", grad_queries, q_full, preferred_element_type=jnp.float32
        )
        grad_attn_in = grad_attn_in + jnp.einsum(
            "te,de->td", key_gradients, key_expanded, preferred_element_type=jnp.float32
        )
        grad_attn_in = grad_attn_in + jnp.einsum(
            "te,de->td", grad_value, v_full, preferred_element_type=jnp.float32
        )
        grad_plain, grad_gain_one = norm_back(
            grad_attn_in, gain_one.astype(jnp.float32), plain_one, scale_one
        )
        input_grads.append(grad_plain + grad_middle)
        dense_terms = (
            grad_query_w,
            grad_key_w,
            grad_value_w,
            grad_out_w,
            grad_router,
            grad_gain_one,
            grad_gain_two,
        )
        expert_terms = (grad_gate_w, grad_up_w, grad_down_w)
        if sums_dense is None:
            sums_dense = dense_terms
            sums_expert = expert_terms
        else:
            sums_dense = jax.tree.map(jnp.add, sums_dense, dense_terms)
            sums_expert = jax.tree.map(jnp.add, sums_expert, expert_terms)
    dense_owned = lax.psum_scatter(sums_dense, ("fsdp", "expert"), scatter_dimension=0, tiled=True)
    expert_owned = jax.tree.map(
        lambda part: part.astype(jnp.float32),
        lax.psum_scatter(as_sent(sums_expert), "fsdp", scatter_dimension=1, tiled=True),
    )
    return (
        jnp.concatenate(outputs, axis=0),
        jnp.concatenate(input_grads, axis=0),
        dense_owned[0],
        dense_owned[1],
        dense_owned[2],
        dense_owned[3],
        dense_owned[4],
        dense_owned[5],
        dense_owned[6],
        expert_owned[0],
        expert_owned[1],
        expert_owned[2],
    )


def solution(mesh):
    in_specs = (
        P(("fsdp", "expert"), None),
        P(("fsdp", "expert"), None),
        P(("fsdp", "expert"), None),
        P(("fsdp", "expert"), None),
        P(("fsdp", "expert"), None),
        P(("fsdp", "expert"), None),
        P(("fsdp", "expert")),
        P(("fsdp", "expert")),
        P("expert", "fsdp", None),
        P("expert", "fsdp", None),
        P("expert", "fsdp", None),
        P(("fsdp", "expert"), None, None),
        P(("fsdp", "expert"), None),
        P(("fsdp", "expert"), None),
    )
    out_specs = (
        P(("fsdp", "expert"), None),
        P(("fsdp", "expert"), None),
        P(("fsdp", "expert"), None),
        P(("fsdp", "expert"), None),
        P(("fsdp", "expert"), None),
        P(("fsdp", "expert"), None),
        P(("fsdp", "expert"), None),
        P(("fsdp", "expert")),
        P(("fsdp", "expert")),
        P("expert", "fsdp", None),
        P("expert", "fsdp", None),
        P("expert", "fsdp", None),
    )
    return jax.shard_map(
        per_device, mesh=mesh, in_specs=in_specs, out_specs=out_specs, check_vma=False
    )
```

profile of v0, /device:TPU:0, one launch (start us, length us, event | category | flops | bytes accessed | tf_op | source)
XLA Modules:
  0.0 2278.9 jit_solution(4387476095432504885)
XLA Ops:
  12.8 42.0 %all-reduce.9 = (bf16[1024]{0:T(1024)(128)(2,1)S(1)}, bf16[1024]{0:T(1024)(128)(2,1)S(1)}) all-reduce(bf16[1024]{0:T(1024)(128)(2,1)S(1)} %dynamic-update-slice, bf16[1024]{0:T(1024)(128)(2,1)S(1)} %dynamic-update-slice.1), channel_id=1, replica_groups=mesh['fsdp'=16,'expert'=2] {'fsdp','expert'}, use_global_device_ids=true, to_apply=%add.4 | all-reduce | flops 2048 | bytes 8192
  69.3 53.9 %all-gather.10.cloned.1.call-done = bf16[1024,512]{1,0:T(8,128)(2,1)} async-done(((bf16[32,512]{1,0:T(8,128)(2,1)}), bf16[1024,512]{1,0:T(8,128)(2,1)}) %all-gather.10.cloned.1.call-update) | async-done | bytes 1048592 | tf_op jit(solution)/shard_map/all_gather | solution.py:83
  125.1 56.5 %all-gather.12.cloned.1.call-done = bf16[1024,1024]{1,0:T(8,128)(2,1)} async-done(((bf16[32,1024]{1,0:T(8,128)(2,1)}), bf16[1024,1024]{1,0:T(8,128)(2,1)}) %all-gather.12.cloned.1.call-update) | async-done | bytes 2097168 | tf_op jit(solution)/shard_map/all_gather | solution.py:82
  186.6 53.0 %all-gather.14.cloned.1.call-done = bf16[1024,1024]{1,0:T(8,128)(2,1)} async-done(((bf16[32,1024]{1,0:T(8,128)(2,1)}), bf16[1024,1024]{1,0:T(8,128)(2,1)}) %all-gather.14.cloned.1.call-update) | async-done | bytes 2097168 | tf_op jit(solution)/shard_map/all_gather | solution.py:85
  261.6 25.6 %all-to-all-done = bf16[2,16,40,1024]{3,2,1,0:T(8,128)(2,1)S(1)} async-done(((bf16[2,16,40,1024]{3,2,1,0:T(8,128)(2,1)}), bf16[2,16,40,1024]{3,2,1,0:T(8,128)(2,1)S(1)}, u32[]{:S(2)}, u32[]{:S(2)}) %all-to-all-start) | async-done | bytes 2621472 | tf_op jit(solution)/shard_map/all_to_all | solution.py:213
  287.2 79.8 %all-gather.16.cloned.1.call-done = bf16[16,1024,512]{2,1,0:T(8,128)(2,1)} async-done(((bf16[16,64,512]{2,1,0:T(8,128)(2,1)}), bf16[16,1024,512]{2,1,0:T(8,128)(2,1)}) %all-gather.16.cloned.1.call-update) | async-done | bytes 16777232 | tf_op jit(solution)/shard_map/all_gather | solution.py:94
  377.3 116.4 %all-gather.18.cloned.1.call-done = bf16[16,1024,512]{2,1,0:T(8,128)(2,1)} async-done(((bf16[16,64,512]{2,1,0:T(8,128)(2,1)}), bf16[16,1024,512]{2,1,0:T(8,128)(2,1)}) %all-gather.18.cloned.1.call-update) | async-done | bytes 16777232 | tf_op jit(solution)/shard_map/all_gather | solution.py:95
  505.2 115.3 %all-gather.20.cloned.1.call-done = bf16[16,512,1024]{2,1,0:T(8,128)(2,1)} async-done(((bf16[16,32,1024]{2,1,0:T(8,128)(2,1)}), bf16[16,512,1024]{2,1,0:T(8,128)(2,1)}) %all-gather.20.cloned.1.call-update) | async-done | bytes 16777232 | tf_op jit(solution)/shard_map/all_gather | solution.py:96
  635.5 89.6 %all_gather.26 = bf16[1024,32]{1,0:T(8,128)(2,1)S(1)} all-gather(bf16[32,32]{1,0:T(8,128)(2,1)S(1)} %copy-done.131), channel_id=1, replica_groups=mesh['fsdp'=16,'expert'=2] {'fsdp','expert'}, dimensions={0}, use_global_device_ids=true | all-gather | bytes 67584 | tf_op jit(solution)/shard_map/all_gather | solution.py:86
  760.8 21.5 all-to-all-done.4
  828.4 22.4 all-to-all-done.5
  868.9 29.6 %all_to_all.40 = bf16[2,16,40,1024]{3,2,1,0:T(8,128)(2,1)S(1)} all-to-all(bf16[2,16,40,1024]{3,2,1,0:T(8,128)(2,1)S(1)} %bitcast.389), channel_id=1, replica_groups=mesh['fsdp'=16,'expert'=2] {'expert'}, dimensions={0} | all-to-all | bytes 5242880 | tf_op jit(solution)/shard_map/all_to_all | solution.py:213
  931.7 25.2 %all-to-all-done.3 = bf16[2,16,40,1024]{3,2,1,0:T(8,128)(2,1)S(1)} async-done(((bf16[2,16,40,1024]{3,2,1,0:T(8,128)(2,1)}), bf16[2,16,40,1024]{3,2,1,0:T(8,128)(2,1)S(1)}, u32[]{:S(2)}, u32[]{:S(2)}) %all-to-all-start.3) | async-done | bytes 2621472 | tf_op jit(solution)/shard_map/all_to_all | solution.py:224
  1003.9 18.4 fusion
  1055.4 21.0 fusion.2
  1142.4 21.1 all-to-all-done.7
  1208.1 60.9 %all-reduce.8 = (f32[1024]{0:T(1024)S(1)}, f32[1024]{0:T(1024)S(1)}) all-reduce(f32[1024]{0:T(1024)S(1)} %add.281, f32[1024]{0:T(1024)S(1)} %copy-done.122), channel_id=7, replica_groups=mesh['fsdp'=16,'expert'=2] {'fsdp','expert'}, use_global_device_ids=true, to_apply=%region_51.55.clone | all-reduce | flops 2048 | bytes 16384
  1276.3 116.6 %reduce-scatter.19.cloned.1.call-done = bf16[16,64,512]{2,1,0:T(8,128)(2,1)} async-done(((bf16[16,1024,512]{2,1,0:T(8,128)(2,1)}), bf16[16,64,512]{2,1,0:T(8,128)(2,1)}) %reduce-scatter.19.cloned.1.call-update) | async-done | bytes 1048592 | tf_op jit(solution)/shard_map/reduce_scatter | solution.py:395
  1395.7 177.6 %reduce-scatter.21.cloned.1.call-done = bf16[16,64,512]{2,1,0:T(8,128)(2,1)} async-done(((bf16[16,1024,512]{2,1,0:T(8,128)(2,1)}), bf16[16,64,512]{2,1,0:T(8,128)(2,1)}) %reduce-scatter.21.cloned.1.call-update) | async-done | bytes 1048592 | tf_op jit(solution)/shard_map/reduce_scatter | solution.py:395
  1576.1 134.9 %reduce-scatter.17.cloned.1.call-done = f32[32,32]{1,0:T(8,128)} async-done(((f32[1024,32]{1,0:T(8,128)}), f32[32,32]{1,0:T(8,128)}) %reduce-scatter.17.cloned.1.call-update) | async-done | bytes 4112 | tf_op jit(solution)/shard_map/reduce_scatter | solution.py:392
  1711.0 137.8 %reduce-scatter.13.cloned.1.call-done = f32[32,512]{1,0:T(8,128)} async-done(((f32[1024,512]{1,0:T(8,128)}), f32[32,512]{1,0:T(8,128)}) %reduce-scatter.13.cloned.1.call-update) | async-done | bytes 65552 | tf_op jit(solution)/shard_map/reduce_scatter | solution.py:392
  1848.7 138.0 %reduce-scatter.11.cloned.1.call-done = f32[32,512]{1,0:T(8,128)} async-done(((f32[1024,512]{1,0:T(8,128)}), f32[32,512]{1,0:T(8,128)}) %reduce-scatter.11.cloned.1.call-update) | async-done | bytes 65552 | tf_op jit(solution)/shard_map/reduce_scatter | solution.py:392
  1986.7 142.1 %reduce-scatter.15.cloned.1.call-done = f32[32,1024]{1,0:T(8,128)} async-done(((f32[1024,1024]{1,0:T(8,128)}), f32[32,1024]{1,0:T(8,128)}) %reduce-scatter.15.cloned.1.call-update) | async-done | bytes 131088 | tf_op jit(solution)/shard_map/reduce_scatter | solution.py:392
  2128.7 143.4 %reduce-scatter.9.cloned.1.call-done = f32[32,1024]{1,0:T(8,128)} async-done(((f32[1024,1024]{1,0:T(8,128)}), f32[32,1024]{1,0:T(8,128)}) %reduce-scatter.9.cloned.1.call-update) | async-done | bytes 131088 | tf_op jit(solution)/shard_map/reduce_scatter | solution.py:392
  (545 shorter events, 419.9 us)
Async XLA Ops:
  7.2 60.3 %all-gather.8.cloned.1.call-start = ((), (), s32[]{:S(2)}) async-start(), calls=%async_computation.16 | async-start | bytes 1081344 | tf_op jit(solution)/shard_map/all_gather | solution.py:84
  8.0 115.2 %all-gather.10.cloned.1.call-start = ((), (), s32[]{:S(2)}) async-start(), calls=%async_computation.17 | async-start | bytes 1081344 | tf_op jit(solution)/shard_map/all_gather | solution.py:83
  8.7 172.8 %all-gather.12.cloned.1.call-start = ((), (), s32[]{:S(2)}) async-start(), calls=%async_computation.18 | async-start | bytes 2162688 | tf_op jit(solution)/shard_map/all_gather | solution.py:82
  9.4 230.2 %all-gather.14.cloned.1.call-start = ((), (), s32[]{:S(2)}) async-start(), calls=%async_computation.19 | async-start | bytes 2162688 | tf_op jit(solution)/shard_map/all_gather | solution.py:85
  10.0 357.0 %all-gather.16.cloned.1.call-start = ((), (), s32[]{:S(2)}) async-start(), calls=%async_computation.20 | async-start | bytes 17825792 | tf_op jit(solution)/shard_map/all_gather | solution.py:94
  10.6 483.1 %all-gather.18.cloned.1.call-start = ((), (), s32[]{:S(2)}) async-start(), calls=%async_computation.21 | async-start | bytes 17825792 | tf_op jit(solution)/shard_map/all_gather | solution.py:95
  11.2 609.4 %all-gather.20.cloned.1.call-start = ((), (), s32[]{:S(2)}) async-start(), calls=%async_computation.22 | async-start | bytes 17825792 | tf_op jit(solution)/shard_map/all_gather | solution.py:96
  54.8 806.7 %copy-start.97 = (f32[1024]{0:T(1024)}, f32[1024]{0:T(1024)S(1)}, u32[]{:S(2)}) copy-start(f32[1024]{0:T(1024)S(1)} %convert_element_type.275) | copy-start | bytes 12292
  54.8 876.8 %copy-start.95 = (s32[128,8]{0,1:T(8,128)}, s32[128,8]{0,1:T(8,128)S(1)}, u32[]{:S(2)}) copy-start(s32[128,8]{0,1:T(8,128)S(1)} %get-tuple-element.79) | copy-start | bytes 12292
  252.2 35.0 %all-to-all-start = ((bf16[2,16,40,1024]{3,2,1,0:T(8,128)(2,1)}), bf16[2,16,40,1024]{3,2,1,0:T(8,128)(2,1)S(1)}, u32[]{:S(2)}, u32[]{:S(2)}) async-start(bf16[2,16,40,1024]{3,2,1,0:T(8,128)(2,1)} %bitcast.387), calls=%async_computation | async-start | bytes 5242880 | tf_op jit(solution)/shard_map/all_to_all | solution.py:213
  631.5 98.8 %all-to-all-start.1 = ((bf16[2,16,40,1024]{3,2,1,0:T(8,128)(2,1)}), bf16[2,16,40,1024]{3,2,1,0:T(8,128)(2,1)S(1)}, u32[]{:S(2)}, u32[]{:S(2)}) async-start(bf16[2,16,40,1024]{3,2,1,0:T(8,128)(2,1)} %copy.147), calls=%async_computation.1 | async-start | bytes 5242880 | tf_op jit(solution)/shard_map/all_to_all | solution.py:224
  748.2 34.1 %all-to-all-start.4 = ((bf16[2,16,40,1024]{3,2,1,0:T(8,128)(2,1)}), bf16[2,16,40,1024]{3,2,1,0:T(8,128)(2,1)}, u32[]{:S(2)}, u32[]{:S(2)}) async-start(bf16[2,16,40,1024]{3,2,1,0:T(8,128)(2,1)} %bitcast.57), calls=%async_computation.4 | async-start | bytes 5242880 | tf_op jit(solution)/shard_map/all_to_all | solution.py:264
  819.2 31.6 %all-to-all-start.5 = ((bf16[2,16,40,1024]{3,2,1,0:T(8,128)(2,1)}), bf16[2,16,40,1024]{3,2,1,0:T(8,128)(2,1)S(1)}, u32[]{:S(2)}, u32[]{:S(2)}) async-start(bf16[2,16,40,1024]{3,2,1,0:T(8,128)(2,1)} %copy.165), calls=%async_computation.5 | async-start | bytes 5242880 | tf_op jit(solution)/shard_map/all_to_all | solution.py:285
  927.1 29.8 %all-to-all-start.3 = ((bf16[2,16,40,1024]{3,2,1,0:T(8,128)(2,1)}), bf16[2,16,40,1024]{3,2,1,0:T(8,128)(2,1)S(1)}, u32[]{:S(2)}, u32[]{:S(2)}) async-start(bf16[2,16,40,1024]{3,2,1,0:T(8,128)(2,1)} %copy.160), calls=%async_computation.3 | async-start | bytes 5242880 | tf_op jit(solution)/shard_map/all_to_all | solution.py:224
  975.2 28.7 %all-to-all-start.6 = ((bf16[2,16,40,1024]{3,2,1,0:T(8,128)(2,1)}), bf16[2,16,40,1024]{3,2,1,0:T(8,128)(2,1)S(1)}, u32[]{:S(2)}, u32[]{:S(2)}) async-start(bf16[2,16,40,1024]{3,2,1,0:T(8,128)(2,1)} %bitcast.388), calls=%async_computation.6 | async-start | bytes 5242880 | tf_op jit(solution)/shard_map/all_to_all | solution.py:264
  979.1 294.4 %reduce-scatter.23.cloned.1.call-start = ((), (), s32[]{:S(2)}) async-start(), calls=%async_computation.30 | async-start | bytes 17825792 | tf_op jit(solution)/shard_map/reduce_scatter | solution.py:395
  1022.4 370.5 %reduce-scatter.19.cloned.1.call-start = ((), (), s32[]{:S(2)}) async-start(), calls=%async_computation.28 | async-start | bytes 17825792 | tf_op jit(solution)/shard_map/reduce_scatter | solution.py:395
  1076.5 496.8 %reduce-scatter.21.cloned.1.call-start = ((), (), s32[]{:S(2)}) async-start(), calls=%async_computation.29 | async-start | bytes 17825792 | tf_op jit(solution)/shard_map/reduce_scatter | solution.py:395
  1136.2 27.4 %all-to-all-start.7 = ((bf16[2,16,40,1024]{3,2,1,0:T(8,128)(2,1)}), bf16[2,16,40,1024]{3,2,1,0:T(8,128)(2,1)S(1)}, u32[]{:S(2)}, u32[]{:S(2)}) async-start(bf16[2,16,40,1024]{3,2,1,0:T(8,128)(2,1)} %copy.174), calls=%async_computation.7 | async-start | bytes 5242880 | tf_op jit(solution)/shard_map/all_to_all | solution.py:285
  1140.2 570.8 %reduce-scatter.17.cloned.1.call-start = ((), (), s32[]{:S(2)}) async-start(), calls=%async_computation.27 | async-start | bytes 540672 | tf_op jit(solution)/shard_map/reduce_scatter | solution.py:392
  1142.2 706.5 %reduce-scatter.13.cloned.1.call-start = ((), (), s32[]{:S(2)}) async-start(), calls=%async_computation.25 | async-start | bytes 2162688 | tf_op jit(solution)/shard_map/reduce_scatter | solution.py:392
  1186.8 799.9 %reduce-scatter.11.cloned.1.call-start = ((), (), s32[]{:S(2)}) async-start(), calls=%async_computation.24 | async-start | bytes 2162688 | tf_op jit(solution)/shard_map/reduce_scatter | solution.py:392
  1192.7 936.1 %reduce-scatter.15.cloned.1.call-start = ((), (), s32[]{:S(2)}) async-start(), calls=%async_computation.26 | async-start | bytes 4325376 | tf_op jit(solution)/shard_map/reduce_scatter | solution.py:392
  1196.6 1075.5 %reduce-scatter.9.cloned.1.call-start = ((), (), s32[]{:S(2)}) async-start(), calls=%async_computation.23 | async-start | bytes 4325376 | tf_op jit(solution)/shard_map/reduce_scatter | solution.py:392
  (149 other events, 3663.8 us)
Sparse Core Ops, SparseCore 0:
  10.9 56.5 all-gather.7
  70.4 52.7 all-gather.9
  126.2 55.3 all-gather.11
  184.4 55.1 all-gather.13
  241.7 125.2 all-gather.15
  369.0 124.6 all-gather.17
  495.9 124.6 all-gather.19
  1022.5 189.6 reduce-scatter.22
  1216.3 176.5 reduce-scatter.18
  1396.8 176.4 reduce-scatter.20
  1576.1 134.8 reduce-scatter.16
  1713.7 135.0 reduce-scatter.12
  1851.6 135.0 reduce-scatter.10
  1989.4 139.3 reduce-scatter.14
  2131.4 140.6 reduce-scatter.8
where the time goes:
time: 2290 us; the launch traced here: 2280 us
  waiting for transfers between devices  1600 us (70%)
  matrix products  281 us (12%)
  blocking collectives  222 us (10%)
  local copies, waits for them, and re-layouts  76.7 us (3%)
  other arithmetic  54.2 us (2%)
  starting transfers between devices  31 us (1%)
    reduce_scatter x5, waiting for transfers between devices, per_device(): lax.psum_scatter(sums_dense, ('fsdp', 'expert'), scatter_dimension=0, til...  696 us
    reduce_scatter x3, waiting for transfers between devices, per_device(): lax.psum_scatter(as_sent(sums_expert), 'fsdp', scatter_dimension=1, tiled...  294 us
    all_gather x1, waiting for transfers between devices, fetch_experts(): lax.all_gather(up_weight, 'fsdp', axis=1, tiled=True)  116 us
    all_gather x1, waiting for transfers between devices, fetch_experts(): lax.all_gather(down_weight, 'fsdp', axis=1, tiled=True)  115 us
    unnamed x2, blocking collectives  103 us
    all_gather x1, blocking collectives, fetch_dense(): lax.all_gather(router_weight, ('fsdp', 'expert'), axis=0, tiled=True)  89.6 us
    all_gather x1, waiting for transfers between devices, fetch_experts(): lax.all_gather(gate_weight, 'fsdp', axis=1, tiled=True)  79.8 us
    all_gather x1, waiting for transfers between devices, fetch_dense(): lax.all_gather(query_weight, ('fsdp', 'expert'), axis=0, tiled=True)  56.5 us
  transfers between devices with their start and end apart: 22, of which 20 were waited for; matrix products, arithmetic and copies ran while one was open for 11% of the time, Pallas kernels for 0%

commit v1 on v0

v1 whole, which is shorter than its diff:
```python
import jax
import jax.numpy as jnp
from jax import lax
from jax.sharding import PartitionSpec as P

MODEL_WIDTH = 1024
QUERY_HEADS = 16
KEY_VALUE_HEADS = 8
HEAD_SIZE = 64
EXPERTS = 32
DEVICE_TOKENS = 128
MB = 2
CAP = 40
ROWS = MB * DEVICE_TOKENS
SLOTS = MB * CAP
Q_COLS = QUERY_HEADS * HEAD_SIZE
KV_COLS = KEY_VALUE_HEADS * HEAD_SIZE
QKV_COLS = Q_COLS + 2 * KV_COLS
SMALL_COLS = 128

EPS = 1e-06
THETA = 10000.0
SCALE = 0.125
HIGH = lax.Precision.HIGHEST
BOTH = ("fsdp", "expert")
F32 = jnp.float32
BF16 = jnp.bfloat16


def mm(spec, a, b):
    return jnp.einsum(spec, a, b, preferred_element_type=F32)


def sequence_layout(seq_lengths, row_number):
    row_index = jnp.arange(row_number, dtype=jnp.int32)
    seq_ends = jnp.cumsum(seq_lengths)
    starts = seq_ends - seq_lengths
    member = (
        (row_index[:, None] >= starts[None, :]) & (row_index[:, None] < seq_ends[None, :])
    ).astype(jnp.int32)
    labels = jnp.arange(seq_lengths.shape[0], dtype=jnp.int32)
    segment = jnp.sum(member * labels[None, :], axis=1)
    offset = jnp.sum(member * starts[None, :], axis=1)
    return (segment, row_index - offset)


def rotary_tables(token_positions):
    half_width = HEAD_SIZE // 2
    frequency = THETA ** (-2.0 * jnp.arange(half_width, dtype=F32) / HEAD_SIZE)
    angles = token_positions.astype(F32)[:, None] * frequency[None, :]
    return jnp.cos(angles)[:, None, :], jnp.sin(angles)[:, None, :]


def rotary_apply(values, cosine, sine_part):
    half_width = HEAD_SIZE // 2
    first_half = values[..., :half_width]
    second_half = values[..., half_width:]
    return jnp.concatenate(
        [
            first_half * cosine - second_half * sine_part,
            second_half * cosine + first_half * sine_part,
        ],
        axis=-1,
    )


def rms_scale(values):
    return lax.rsqrt(jnp.mean(values * values, axis=1, keepdims=True) + EPS)


def norm_back(grad_normed, gain_vec, plain_part, scale_part):
    grad_gain = jnp.sum(grad_normed * plain_part, axis=0)
    shaped = grad_normed * gain_vec[None, :]
    grad_input = scale_part * (
        shaped - plain_part * jnp.mean(shaped * plain_part, axis=1, keepdims=True)
    )
    return (grad_input, grad_gain)


def fsdp_groups(local_experts):
    size = lax.axis_size("fsdp")
    runs = size // local_experts
    if runs == 1:
        return None, None
    inner = [[s * local_experts + j for j in range(local_experts)] for s in range(runs)]
    cross = [[s * local_experts + j for s in range(runs)] for j in range(local_experts)]
    return inner, cross


def weight_to_expert(weight, inner, cross):
    part = lax.all_to_all(
        weight, "fsdp", split_axis=0, concat_axis=1, axis_index_groups=inner, tiled=True
    )[0]
    if cross is not None:
        part = lax.all_gather(part, "fsdp", axis=0, axis_index_groups=cross, tiled=True)
    return part


def grad_to_owners(grad, inner, cross):
    if cross is not None:
        grad = lax.psum_scatter(
            grad, "fsdp", scatter_dimension=0, axis_index_groups=cross, tiled=True
        )
    return lax.all_to_all(
        grad.astype(BF16)[None],
        "fsdp",
        split_axis=1,
        concat_axis=0,
        axis_index_groups=inner,
        tiled=True,
    ).astype(F32)


def exchange(rows, local_experts, inner):
    if inner is None:
        return lax.all_to_all(rows, BOTH, split_axis=0, concat_axis=0, tiled=True)
    groups = EXPERTS // local_experts
    shaped = rows.reshape((local_experts, groups) + rows.shape[1:])
    shaped = lax.all_to_all(
        shaped, "fsdp", split_axis=0, concat_axis=0, axis_index_groups=inner, tiled=True
    )
    shaped = lax.all_to_all(shaped, "expert", split_axis=1, concat_axis=1, tiled=True)
    return shaped.reshape(rows.shape)


def per_device(
    tokens,
    query_weight,
    key_projection,
    value_projection,
    output_weight,
    router_weight,
    attn_gain,
    ffn_gain,
    gate_weight,
    up_weight,
    down_weight,
    lengths,
    routes,
    cotangent,
):
    local_experts = gate_weight.shape[0]
    groups = EXPERTS // local_experts
    inner, cross = fsdp_groups(local_experts)
    heads = QUERY_HEADS // KEY_VALUE_HEADS

    small = jnp.concatenate(
        [
            router_weight,
            attn_gain[:, None],
            ffn_gain[:, None],
            jnp.zeros((router_weight.shape[0], SMALL_COLS - EXPERTS - 2), BF16),
        ],
        axis=1,
    )
    packed = jnp.concatenate(
        [query_weight, key_projection, value_projection, output_weight, small], axis=1
    )
    full = lax.all_gather(packed, BOTH, axis=0, tiled=True)
    qkv_full = full[:, :QKV_COLS]
    o_full = full[:, QKV_COLS : QKV_COLS + MODEL_WIDTH]
    small_full = full[:, QKV_COLS + MODEL_WIDTH :]
    r_full = small_full[:, :EXPERTS]
    gain_one = small_full[:, EXPERTS].astype(F32)
    gain_two = small_full[:, EXPERTS + 1].astype(F32)
    gate_full = weight_to_expert(gate_weight, inner, cross)
    up_full = weight_to_expert(up_weight, inner, cross)
    down_full = weight_to_expert(down_weight, inner, cross)

    plain_in = tokens.astype(F32)
    grad_out = cotangent.astype(F32)
    layouts = [sequence_layout(lengths[0, b], DEVICE_TOKENS) for b in range(MB)]
    segment = jnp.stack([s for s, _ in layouts])
    cosine, sine = rotary_tables(jnp.concatenate([p for _, p in layouts]))
    row_index = jnp.arange(DEVICE_TOKENS, dtype=jnp.int32)
    allowed = (segment[:, :, None] == segment[:, None, :]) & (
        row_index[:, None] >= row_index[None, :]
    )[None]

    local = jnp.arange(EXPERTS, dtype=jnp.int32)
    named = (local % groups) * local_experts + local // groups
    hits = jnp.any(routes[:, :, None] == named[None, None, :], axis=1)
    all_rows = jnp.arange(ROWS, dtype=jnp.int32)
    below = (all_rows[:, None] > all_rows[None, :]).astype(BF16)
    rank = mm("ts,se->te", below, hits.astype(BF16)).astype(jnp.int32)
    rank = jnp.where(hits, rank, -1)
    slot_id = jnp.arange(SLOTS, dtype=jnp.int32)
    place = rank.T[:, None, :] == slot_id[None, :, None]
    place_rows = place.astype(BF16).reshape(EXPERTS * SLOTS, ROWS)

    scale_one = rms_scale(plain_in)
    plain_one = plain_in * scale_one
    attention_input = (plain_one * gain_one[None, :]).astype(BF16)
    qkv = mm("td,de->te", attention_input, qkv_full)
    query = (
        rotary_apply(qkv[:, :Q_COLS].reshape(ROWS, QUERY_HEADS, HEAD_SIZE), cosine, sine)
        .astype(BF16)
        .reshape(MB, DEVICE_TOKENS, KEY_VALUE_HEADS, heads, HEAD_SIZE)
    )
    key = (
        rotary_apply(
            qkv[:, Q_COLS : Q_COLS + KV_COLS].reshape(ROWS, KEY_VALUE_HEADS, HEAD_SIZE),
            cosine,
            sine,
        )
        .astype(BF16)
        .reshape(MB, DEVICE_TOKENS, KEY_VALUE_HEADS, HEAD_SIZE)
    )
    value = (
        qkv[:, Q_COLS + KV_COLS :]
        .astype(BF16)
        .reshape(MB, DEVICE_TOKENS, KEY_VALUE_HEADS, HEAD_SIZE)
    )
    scores = mm("bqgrd,bkgd->bgrqk", query, key) * SCALE
    scores = jnp.where(allowed[:, None, None], scores, -1e30)
    exp_scores = jnp.exp(scores - jnp.max(scores, axis=-1, keepdims=True))
    probs = exp_scores / jnp.sum(exp_scores, axis=-1, keepdims=True)
    probs_low = probs.astype(BF16)
    mixed = mm("bgrqk,bkgd->bqgrd", probs_low, value).reshape(ROWS, Q_COLS).astype(BF16)
    middle = plain_in + mm("te,ed->td", mixed, o_full)
    scale_two = rms_scale(middle)
    plain_two = middle * scale_two
    ffn_in = (plain_two * gain_two[None, :]).astype(BF16)

    dispatch = mm("st,td->sd", place_rows, ffn_in).astype(BF16)
    received = exchange(
        dispatch.reshape(EXPERTS, SLOTS, MODEL_WIDTH), local_experts, inner
    ).reshape(EXPERTS * SLOTS, MODEL_WIDTH)

    logits = mm("td,de->te", ffn_in, r_full)
    logits = logits.reshape(ROWS, groups, local_experts).swapaxes(1, 2).reshape(ROWS, EXPERTS)
    logits = jnp.where(hits, logits, -jnp.inf)
    exp_logits = jnp.exp(logits - jnp.max(logits, axis=1, keepdims=True))
    gates = exp_logits / jnp.sum(exp_logits, axis=1, keepdims=True)
    slot_gates = jnp.sum(jnp.where(place, gates.T[:, None, :], 0.0), axis=2)

    cot_rows = mm("st,td->sd", place_rows, cotangent).reshape(EXPERTS, SLOTS, MODEL_WIDTH)
    grad_recv = exchange(
        (slot_gates[:, :, None] * cot_rows).astype(BF16), local_experts, inner
    ).reshape(EXPERTS * SLOTS, MODEL_WIDTH)

    gate_act = mm("sd,dh->sh", received, gate_full)
    up_act = mm("sd,dh->sh", received, up_full)
    sigmoid_g = jax.nn.sigmoid(gate_act)
    silu_gate = gate_act * sigmoid_g
    hidden = (silu_gate * up_act).astype(BF16)
    produced = mm("sh,hd->sd", hidden, down_full).astype(BF16)
    returned = exchange(
        produced.reshape(EXPERTS, SLOTS, MODEL_WIDTH), local_experts, inner
    ).reshape(EXPERTS * SLOTS, MODEL_WIDTH)

    grad_hidden = mm("sd,hd->sh", grad_recv, down_full)
    grad_gact = (
        grad_hidden * up_act * sigmoid_g * (1.0 + gate_act * (1.0 - sigmoid_g))
    ).astype(BF16)
    grad_uact = (grad_hidden * silu_gate).astype(BF16)
    grad_inputs = (
        mm("sh,dh->sd", grad_gact, gate_full) + mm("sh,dh->sd", grad_uact, up_full)
    ).astype(BF16)
    grad_back = exchange(
        grad_inputs.reshape(EXPERTS, SLOTS, MODEL_WIDTH), local_experts, inner
    ).reshape(EXPERTS * SLOTS, MODEL_WIDTH)
    grad_down = grad_to_owners(mm("sh,sd->hd", hidden, grad_recv), inner, cross)
    grad_gate = grad_to_owners(mm("sd,sh->dh", received, grad_gact), inner, cross)
    grad_up = grad_to_owners(mm("sd,sh->dh", received, grad_uact), inner, cross)

    slot_column = slot_gates.reshape(EXPERTS * SLOTS, 1)
    part_one = slot_column.astype(BF16)
    rest = slot_column - part_one.astype(F32)
    part_two = rest.astype(BF16)
    part_three = (rest - part_two.astype(F32)).astype(BF16)
    combined = (
        mm("st,sd->td", place_rows * part_three, returned)
        + mm("st,sd->td", place_rows * part_two, returned)
    ) + mm("st,sd->td", place_rows * part_one, returned)
    layer_out = (middle + combined).astype(BF16)

    products = mm("sd,td->st", returned, cotangent).reshape(EXPERTS, SLOTS, ROWS)
    grad_gates = jnp.sum(jnp.where(place, products, 0.0), axis=1).T
    grad_logits = gates * (grad_gates - jnp.sum(gates * grad_gates, axis=1, keepdims=True))
    grad_logits = (
        grad_logits.reshape(ROWS, local_experts, groups).swapaxes(1, 2).reshape(ROWS, EXPERTS)
    )
    grad_router = jnp.dot(ffn_in.astype(F32).T, grad_logits, precision=HIGH)
    grad_ffn_in = jnp.dot(grad_logits, r_full.astype(F32).T, precision=HIGH)
    grad_ffn_in = grad_ffn_in + mm("st,sd->td", place_rows, grad_back)
    grad_middle, grad_gain_two = norm_back(grad_ffn_in, gain_two, plain_two, scale_two)
    grad_middle = grad_middle + grad_out
    grad_attn = grad_middle.astype(BF16)
    grad_o = lax.psum_scatter(
        mm("te,td->ed", mixed, grad_attn), BOTH, scatter_dimension=0, tiled=True
    )
    grad_mix = (
        mm("td,ed->te", grad_attn, o_full)
        .astype(BF16)
        .reshape(MB, DEVICE_TOKENS, KEY_VALUE_HEADS, heads, HEAD_SIZE)
    )
    grad_value = mm("bgrqk,bqgrd->bkgd", probs_low, grad_mix).astype(BF16).reshape(ROWS, KV_COLS)
    grad_probs = mm("bqgrd,bkgd->bgrqk", grad_mix, value)
    row_inner = jnp.sum(probs * grad_probs, axis=-1, keepdims=True)
    grad_scores = (probs * (grad_probs - row_inner)).astype(BF16)
    grad_query = mm("bgrqk,bkgd->bqgrd", grad_scores, key) * SCALE
    grad_query = (
        rotary_apply(grad_query.reshape(ROWS, QUERY_HEADS, HEAD_SIZE), cosine, -sine)
        .astype(BF16)
        .reshape(ROWS, Q_COLS)
    )
    grad_key = mm("bgrqk,bqgrd->bkgd", grad_scores, query) * SCALE
    grad_key = (
        rotary_apply(grad_key.reshape(ROWS, KEY_VALUE_HEADS, HEAD_SIZE), cosine, -sine)
        .astype(BF16)
        .reshape(ROWS, KV_COLS)
    )
    grad_qkv = jnp.concatenate([grad_query, grad_key, grad_value], axis=1)
    grad_qkv_w = lax.psum_scatter(
        mm("td,te->de", attention_input, grad_qkv), BOTH, scatter_dimension=0, tiled=True
    )
    grad_attn_in = mm("te,de->td", grad_qkv, qkv_full)
    grad_plain, grad_gain_one = norm_back(grad_attn_in, gain_one, plain_one, scale_one)
    small_grads = jnp.concatenate(
        [
            grad_router,
            grad_gain_one[:, None],
            grad_gain_two[:, None],
            jnp.zeros((MODEL_WIDTH, SMALL_COLS - EXPERTS - 2), F32),
        ],
        axis=1,
    )
    small_owned = lax.psum_scatter(small_grads, BOTH, scatter_dimension=0, tiled=True)
    return (
        layer_out,
        grad_plain + grad_middle,
        grad_qkv_w[:, :Q_COLS],
        grad_qkv_w[:, Q_COLS : Q_COLS + KV_COLS],
        grad_qkv_w[:, Q_COLS + KV_COLS :],
        grad_o,
        small_owned[:, :EXPERTS],
        small_owned[:, EXPERTS],
        small_owned[:, EXPERTS + 1],
        grad_gate,
        grad_up,
        grad_down,
    )


def solution(mesh):
    in_specs = (
        P(("fsdp", "expert"), None),
        P(("fsdp", "expert"), None),
        P(("fsdp", "expert"), None),
        P(("fsdp", "expert"), None),
        P(("fsdp", "expert"), None),
        P(("fsdp", "expert"), None),
        P(("fsdp", "expert")),
        P(("fsdp", "expert")),
        P("expert", "fsdp", None),
        P("expert", "fsdp", None),
        P("expert", "fsdp", None),
        P(("fsdp", "expert"), None, None),
        P(("fsdp", "expert"), None),
        P(("fsdp", "expert"), None),
    )
    out_specs = (
        P(("fsdp", "expert"), None),
        P(("fsdp", "expert"), None),
        P(("fsdp", "expert"), None),
        P(("fsdp", "expert"), None),
        P(("fsdp", "expert"), None),
        P(("fsdp", "expert"), None),
        P(("fsdp", "expert"), None),
        P(("fsdp", "expert")),
        P(("fsdp", "expert")),
        P("expert", "fsdp", None),
        P("expert", "fsdp", None),
        P("expert", "fsdp", None),
    )
    return jax.shard_map(
        per_device, mesh=mesh, in_specs=in_specs, out_specs=out_specs, check_vma=False
    )
```

time: 2290 us -> 1170 us (0.51)
  waiting for transfers between devices: 1600 us -> 833 us
  blocking collectives: 222 us -> 0 us
  matrix products: 281 us -> 128 us
  starting transfers between devices: 31 us -> 69.1 us
    reduce_scatter x8 -> x3, waiting for transfers between devices: 990 us -> 322 us  [the longest x1 178 us: per_device(): lax.psum_scatter(mm('td,te->de', attention_input, grad_qkv), BOTH, scatte...]
    all_gather x7 -> x1, waiting for transfers between devices: 479 us -> 49.8 us  [per_device(): full = lax.all_gather(packed, BOTH, axis=0, tiled=True)]
    all_to_all x7 -> x10, waiting for transfers between devices: 123 us -> 461 us  [the longest x4 417 us: exchange(): return lax.all_to_all(rows, BOTH, split_axis=0, concat_axis=0, tiled=True)]
    dot_general x60 -> x31, matrix products: 281 us -> 126 us  [the longest x29 124 us: mm(): return jnp.einsum(spec, a, b, preferred_element_type=F32)]
    unnamed x2 -> x0, blocking collectives: 103 us -> none
    all_gather x1 -> x0, blocking collectives: 89.6 us -> none  [fetch_dense(): lax.all_gather(router_weight, ('fsdp', 'expert'), axis=0, tiled=True)]
    gather x8 -> x0, local copies, waits for them, and re-layouts: 40.9 us -> none  [the longest x2 10.7 us: per_device(): jnp.take(grad_back, slot_of, axis=0)]
    all_to_all x1 -> x0, blocking collectives: 29.6 us -> none  [per_device(): lax.all_to_all(dispatch_rows, 'expert', split_axis=0, concat_axis=0, tile...]
  transfers between devices with their start and end apart: 22 -> 14, of which waited for: 20 -> 11; matrix products, arithmetic and copies ran while one was open for 11% -> 15% of each run, Pallas kernels for 0% -> 0%
where the time goes in v1:
time: 1170 us; the launch traced here: 1160 us
  waiting for transfers between devices  833 us (71%)
  matrix products  128 us (11%)
  local copies, waits for them, and re-layouts  76.6 us (7%)
  starting transfers between devices  69.1 us (6%)
  other arithmetic  37.8 us (3%)
  between operations  15 us (1%)
    all_to_all x4, waiting for transfers between devices, exchange(): return lax.all_to_all(rows, BOTH, split_axis=0, concat_axis=0, tiled=True)  417 us
    reduce_scatter x1, waiting for transfers between devices, per_device(): lax.psum_scatter(mm('td,te->de', attention_input, grad_qkv), BOTH, scatte...  178 us
    reduce_scatter x1, waiting for transfers between devices, per_device(): lax.psum_scatter(mm('te,td->ed', mixed, grad_attn), BOTH, scatter_dimensi...  144 us
    dot_general x29, matrix products, mm(): return jnp.einsum(spec, a, b, preferred_element_type=F32)  124 us
    all_gather x1, waiting for transfers between devices, per_device(): full = lax.all_gather(packed, BOTH, axis=0, tiled=True)  49.8 us
    unnamed x64, local copies, waits for them, and re-layouts  37 us
    all_to_all x3, waiting for transfers between devices, weight_to_expert(): lax.all_to_all(weight, 'fsdp', split_axis=0, concat_axis=1, axis_index_gr...  37 us
    unnamed x4, other arithmetic  27.1 us
  transfers between devices with their start and end apart: 14, of which 11 were waited for; matrix products, arithmetic and copies ran while one was open for 15% of the time, Pallas kernels for 0%

profile of v1, /device:TPU:0, one launch (start us, length us, event | category | flops | bytes accessed | tf_op | source)
XLA Modules:
  0.0 1160.2 jit_solution(18380687589397764474)
XLA Ops:
  10.5 7.4 all-to-all-start.1
  19.5 25.6 %all-to-all-done.1 = bf16[16,64,512]{2,1,0:T(8,128)(2,1)S(1)} async-done(((bf16[16,64,512]{2,1,0:T(8,128)(2,1)}), bf16[16,64,512]{2,1,0:T(8,128)(2,1)S(1)}, u32[]{:S(2)}, u32[]{:S(2)}) %all-to-all-start.1) | async-done | bytes 1048608 | tf_op jit(solution)/shard_map/all_to_all | solution.py:91
  45.1 6.8 all-to-all-start.2
  52.9 49.8 %all-gather.2.cloned.1.call-done = bf16[1024,3200]{1,0:T(8,128)(2,1)} async-done(((bf16[32,3200]{1,0:T(8,128)(2,1)}), bf16[1024,3200]{1,0:T(8,128)(2,1)}) %all-gather.2.cloned.1.call-update) | async-done | bytes 6553616 | tf_op jit(solution)/shard_map/all_gather | solution.py:159
  128.2 11.4 all-to-all-done.3
  139.5 6.5 all-to-all-start
  151.3 110.8 %all-to-all-done = bf16[32,80,1024]{2,1,0:T(8,128)(2,1)} async-done(((bf16[32,80,1024]{2,1,0:T(8,128)(2,1)}), bf16[32,80,1024]{2,1,0:T(8,128)(2,1)}, u32[]{:S(2)}, u32[]{:S(2)}) %all-to-all-start) | async-done | bytes 5242912 | tf_op jit(solution)/shard_map/all_to_all | solution.py:116
  267.1 8.1 fusion.122
  275.2 7.2 fusion.121
  282.4 100.9 %all-to-all-done.5 = bf16[32,80,1024]{2,1,0:T(8,128)(2,1)} async-done(((bf16[32,80,1024]{2,1,0:T(8,128)(2,1)}), bf16[32,80,1024]{2,1,0:T(8,128)(2,1)}, u32[]{:S(2)}, u32[]{:S(2)}) %all-to-all-start.5) | async-done | bytes 5242912 | tf_op jit(solution)/shard_map/all_to_all | solution.py:116
  383.2 12.0 %multiply_convert_fusion.1 = (bf16[2560,512]{1,0:T(8,128)(2,1)}, bf16[2560,512]{1,0:T(8,128)(2,1)}, bf16[2560,512]{1,0:T(8,128)(2,1)S(1)}) fusion(f32[2560,512]{1,0:T(8,128)} %fusion.121, f32[2560,512]{1,0:T(8,128)} %fusion.122, bf16[2560,1024]{1,0:T(8,128)(2,1)} %bitcast.37, bf16[512,1024]{1,0:T(8,128)(2,1)} %bitcast.26), kind=kOutput, calls=%fused_computation.5 | convolution fusion | flops 2704015360 | bytes 24641536 | tf_op jit(solution)/shard_map/sd,hd->sh/dot_general | solution.py:31
  395.2 6.5 convolution_convert_fusion.1
  417.8 104.9 %all-to-all-done.4 = bf16[32,80,1024]{2,1,0:T(8,128)(2,1)} async-done(((bf16[32,80,1024]{2,1,0:T(8,128)(2,1)}), bf16[32,80,1024]{2,1,0:T(8,128)(2,1)}, u32[]{:S(2)}, u32[]{:S(2)}) %all-to-all-start.4) | async-done | bytes 5242912 | tf_op jit(solution)/shard_map/all_to_all | solution.py:116
  527.4 10.0 reduce-scatter.8.cloned.1.call-start
  542.9 100.6 %all-to-all-done.6 = bf16[32,80,1024]{2,1,0:T(8,128)(2,1)} async-done(((bf16[32,80,1024]{2,1,0:T(8,128)(2,1)}), bf16[32,80,1024]{2,1,0:T(8,128)(2,1)}, u32[]{:S(2)}, u32[]{:S(2)}) %all-to-all-start.6) | async-done | bytes 5242912 | tf_op jit(solution)/shard_map/all_to_all | solution.py:116
  692.8 6.2 fusion.22
  702.4 9.0 reduce.10
  721.7 6.2 fusion.23
  730.9 9.0 reduce.11
  742.6 6.7 all-to-all-start.8
  758.4 9.0 reduce.12
  772.2 7.6 all-to-all-start.9
  828.0 177.9 %reduce-scatter.4.cloned.1.call-done = f32[32,2048]{1,0:T(8,128)} async-done(((f32[1024,2048]{1,0:T(8,128)}), f32[32,2048]{1,0:T(8,128)}) %reduce-scatter.4.cloned.1.call-update) | async-done | bytes 262160 | tf_op jit(solution)/shard_map/reduce_scatter | solution.py:315
  1009.0 144.3 %reduce-scatter.6.cloned.1.call-done = f32[32,1024]{1,0:T(8,128)} async-done(((f32[1024,1024]{1,0:T(8,128)}), f32[32,1024]{1,0:T(8,128)}) %reduce-scatter.6.cloned.1.call-update) | async-done | bytes 131088 | tf_op jit(solution)/shard_map/reduce_scatter | solution.py:290
  (187 shorter events, 200.8 us)
Async XLA Ops:
  7.2 10.8 copy-start.22
  7.2 11.2 copy-start.21
  7.2 12.1 %copy-start = (bf16[256,1024]{1,0:T(8,128)(2,1)S(1)}, bf16[256,1024]{1,0:T(8,128)(2,1)}, u32[]{:S(2)}) copy-start(bf16[256,1024]{1,0:T(8,128)(2,1)} %param.14) | copy-start | bytes 1572868
  7.2 95.5 %all-gather.2.cloned.1.call-start = ((), (), s32[]{:S(2)}) async-start(), calls=%async_computation.13 | async-start | bytes 6758400 | tf_op jit(solution)/shard_map/all_gather | solution.py:159
  10.5 34.6 %all-to-all-start.1 = ((bf16[16,64,512]{2,1,0:T(8,128)(2,1)}), bf16[16,64,512]{2,1,0:T(8,128)(2,1)S(1)}, u32[]{:S(2)}, u32[]{:S(2)}) async-start(bf16[16,64,512]{2,1,0:T(8,128)(2,1)} %param.22), calls=%async_computation.1 | async-start | bytes 2097152 | tf_op jit(solution)/shard_map/all_to_all | solution.py:91
  45.1 62.5 %copy-start.9 = (bf16[16,64,512]{2,1,0:T(8,128)(2,1)}, bf16[16,64,512]{2,1,0:T(8,128)(2,1)S(1)}, u32[]{:S(2)}) copy-start(bf16[16,64,512]{2,1,0:T(8,128)(2,1)S(1)} %all-to-all-done.1) | copy-start | bytes 3145732
  45.1 67.1 %all-to-all-start.2 = ((bf16[16,64,512]{2,1,0:T(8,128)(2,1)}), bf16[16,64,512]{2,1,0:T(8,128)(2,1)}, u32[]{:S(2)}, u32[]{:S(2)}) async-start(bf16[16,64,512]{2,1,0:T(8,128)(2,1)} %param.23), calls=%async_computation.2 | async-start | bytes 2097152 | tf_op jit(solution)/shard_map/all_to_all | solution.py:91
  52.0 55.7 %copy-start.19 = (f32[256]{0:T(256)}, f32[256]{0:T(256)S(1)}, u32[]{:S(2)}) copy-start(f32[256]{0:T(256)S(1)} %add_rsqrt_fusion.1) | copy-start | bytes 3076
  112.3 27.2 %all-to-all-start.3 = ((bf16[16,32,1024]{2,1,0:T(8,128)(2,1)}), bf16[16,32,1024]{2,1,0:T(8,128)(2,1)}, u32[]{:S(2)}, u32[]{:S(2)}) async-start(bf16[16,32,1024]{2,1,0:T(8,128)(2,1)} %param.24), calls=%async_computation.3 | async-start | bytes 2097152 | tf_op jit(solution)/shard_map/all_to_all | solution.py:91
  139.5 8.6 copy-start.14
  139.5 122.6 %all-to-all-start = ((bf16[32,80,1024]{2,1,0:T(8,128)(2,1)}), bf16[32,80,1024]{2,1,0:T(8,128)(2,1)}, u32[]{:S(2)}, u32[]{:S(2)}) async-start(bf16[32,80,1024]{2,1,0:T(8,128)(2,1)} %bitcast.233), calls=%async_computation | async-start | bytes 10485760 | tf_op jit(solution)/shard_map/all_to_all | solution.py:116
  262.1 121.1 %all-to-all-start.5 = ((bf16[32,80,1024]{2,1,0:T(8,128)(2,1)}), bf16[32,80,1024]{2,1,0:T(8,128)(2,1)}, u32[]{:S(2)}, u32[]{:S(2)}) async-start(bf16[32,80,1024]{2,1,0:T(8,128)(2,1)} %multiply_convert_fusion), calls=%async_computation.5 | async-start | bytes 10485760 | tf_op jit(solution)/shard_map/all_to_all | solution.py:116
  267.1 8.1 copy-start.10
  395.2 6.6 copy-start.25
  401.8 120.9 %all-to-all-start.4 = ((bf16[32,80,1024]{2,1,0:T(8,128)(2,1)}), bf16[32,80,1024]{2,1,0:T(8,128)(2,1)}, u32[]{:S(2)}, u32[]{:S(2)}) async-start(bf16[32,80,1024]{2,1,0:T(8,128)(2,1)} %bitcast.241), calls=%async_computation.4 | async-start | bytes 10485760 | tf_op jit(solution)/shard_map/all_to_all | solution.py:116
  522.7 120.9 %all-to-all-start.6 = ((bf16[32,80,1024]{2,1,0:T(8,128)(2,1)}), bf16[32,80,1024]{2,1,0:T(8,128)(2,1)}, u32[]{:S(2)}, u32[]{:S(2)}) async-start(bf16[32,80,1024]{2,1,0:T(8,128)(2,1)} %bitcast.240), calls=%async_computation.6 | async-start | bytes 10485760 | tf_op jit(solution)/shard_map/all_to_all | solution.py:116
  527.4 299.1 %reduce-scatter.8.cloned.1.call-start = ((), (), s32[]{:S(2)}) async-start(), calls=%async_computation.16 | async-start | bytes 540672 | tf_op jit(solution)/shard_map/reduce_scatter | solution.py:329
  542.9 104.7 %copy-start.18 = (f32[256]{0:T(256)S(1)}, f32[256]{0:T(256)}, u32[]{:S(2)}) copy-start(f32[256]{0:T(256)} %copy-done.17) | copy-start | bytes 3076
  686.5 319.4 %reduce-scatter.4.cloned.1.call-start = ((), (), s32[]{:S(2)}) async-start(), calls=%async_computation.14 | async-start | bytes 8650752 | tf_op jit(solution)/shard_map/reduce_scatter | solution.py:315
  711.4 7.5 copy-start.5
  714.1 28.4 %all-to-all-start.7 = ((bf16[16,2,16384]{2,1,0:T(2,128)(2,1)}), bf16[16,2,16384]{2,1,0:T(2,128)(2,1)}, u32[]{:S(2)}, u32[]{:S(2)}) async-start(bf16[16,2,16384]{2,1,0:T(2,128)(2,1)} %reshape.475), calls=%async_computation.10 | async-start | bytes 2097152 | tf_op jit(solution)/shard_map/all_to_all | solution.py:104
  718.9 434.4 %reduce-scatter.6.cloned.1.call-start = ((), (), s32[]{:S(2)}) async-start(), calls=%async_computation.15 | async-start | bytes 4325376 | tf_op jit(solution)/shard_map/reduce_scatter | solution.py:290
  742.6 29.7 %all-to-all-start.8 = ((bf16[16,2,16384]{2,1,0:T(2,128)(2,1)}), bf16[16,2,16384]{2,1,0:T(2,128)(2,1)}, u32[]{:S(2)}, u32[]{:S(2)}) async-start(bf16[16,2,16384]{2,1,0:T(2,128)(2,1)} %reshape.477), calls=%async_computation.11 | async-start | bytes 2097152 | tf_op jit(solution)/shard_map/all_to_all | solution.py:104
  772.2 30.5 %all-to-all-start.9 = ((bf16[16,2,16384]{2,1,0:T(2,128)(2,1)}), bf16[16,2,16384]{2,1,0:T(2,128)(2,1)}, u32[]{:S(2)}, u32[]{:S(2)}) async-start(bf16[16,2,16384]{2,1,0:T(2,128)(2,1)} %reshape.479), calls=%async_computation.12 | async-start | bytes 2097152 | tf_op jit(solution)/shard_map/all_to_all | solution.py:104
  (16 other events, 50.4 us)
Sparse Core Ops, SparseCore 0:
  11.5 91.1 all-gather.1
  686.6 137.7 reduce-scatter.7
  826.7 179.0 reduce-scatter.3
  1008.6 144.6 reduce-scatter.5

commit v2 on v1

--- a/solution.py
+++ b/solution.py
@@ -121,6 +121,13 @@
     )
     shaped = lax.all_to_all(shaped, "expert", split_axis=1, concat_axis=1, tiled=True)
     return shaped.reshape(rows.shape)
+
+
+def sum_to_owners(grad):
+    devices = lax.axis_size(BOTH)
+    parts = grad.reshape(devices, grad.shape[0] // devices, grad.shape[1])
+    parts = lax.all_to_all(parts, BOTH, split_axis=0, concat_axis=0, tiled=True)
+    return jnp.sum(parts.astype(F32), axis=0)
 
 
 def per_device(
@@ -287,9 +294,7 @@
     grad_middle, grad_gain_two = norm_back(grad_ffn_in, gain_two, plain_two, scale_two)
     grad_middle = grad_middle + grad_out
     grad_attn = grad_middle.astype(BF16)
-    grad_o = lax.psum_scatter(
-        mm("te,td->ed", mixed, grad_attn), BOTH, scatter_dimension=0, tiled=True
-    )
+    grad_o = sum_to_owners(mm("te,td->ed", mixed, grad_attn).astype(BF16))
     grad_mix = (
         mm("td,ed->te", grad_attn, o_full)
         .astype(BF16)
@@ -312,9 +317,7 @@
         .reshape(ROWS, KV_COLS)
     )
     grad_qkv = jnp.concatenate([grad_query, grad_key, grad_value], axis=1)
-    grad_qkv_w = lax.psum_scatter(
-        mm("td,te->de", attention_input, grad_qkv), BOTH, scatter_dimension=0, tiled=True
-    )
+    grad_qkv_w = mm("td,te->de", attention_input, grad_qkv).astype(BF16)
     grad_attn_in = mm("te,de->td", grad_qkv, qkv_full)
     grad_plain, grad_gain_one = norm_back(grad_attn_in, gain_one, plain_one, scale_one)
     small_grads = jnp.concatenate(
@@ -322,11 +325,17 @@
             grad_router,
             grad_gain_one[:, None],
             grad_gain_two[:, None],
-            jnp.zeros((MODEL_WIDTH, SMALL_COLS - EXPERTS - 2), F32),
+            jnp.zeros((MODEL_WIDTH, SMALL_COLS // 2 - EXPERTS - 2), F32),
         ],
         axis=1,
     )
-    small_owned = lax.psum_scatter(small_grads, BOTH, scatter_dimension=0, tiled=True)
+    small_high = small_grads.astype(BF16)
+    small_low = (small_grads - small_high.astype(F32)).astype(BF16)
+    owned = sum_to_owners(jnp.concatenate([grad_qkv_w, small_high, small_low], axis=1))
+    small_owned = (
+        owned[:, QKV_COLS : QKV_COLS + SMALL_COLS // 2] + owned[:, QKV_COLS + SMALL_COLS // 2 :]
+    )
+    grad_qkv_w = owned[:, :QKV_COLS]
     return (
         layer_out,
         grad_plain + grad_middle,

time: 1170 us -> 924 us (0.79)
  waiting for transfers between devices: 833 us -> 593 us
    reduce_scatter x3 -> x0, waiting for transfers between devices: 322 us -> none  [the longest x1 178 us: per_device(): lax.psum_scatter(mm('td,te->de', attention_input, grad_qkv), BOTH, scatte...]
    all_to_all x0 -> x2, waiting for transfers between devices: none -> 67.2 us  [sum_to_owners(): parts = lax.all_to_all(parts, BOTH, split_axis=0, concat_axis=0, tiled=True)]
    all_to_all x3, waiting for transfers between devices: 7.2 us -> 30.2 us  [grad_to_owners(): lax.all_to_all(grad.astype(BF16)[None], 'fsdp', split_axis=1, concat_axis...]
    unnamed x64 -> x106, local copies, waits for them, and re-layouts: 37 us -> 35.7 us
  transfers between devices with their start and end apart: 14 -> 13, of which waited for: 11 -> 12; matrix products, arithmetic and copies ran while one was open for 15% -> 21% of each run, Pallas kernels for 0% -> 0%
where the time goes in v2:
time: 924 us; the launch traced here: 914 us
  waiting for transfers between devices  593 us (64%)
  matrix products  126 us (14%)
  local copies, waits for them, and re-layouts  70.4 us (8%)
  starting transfers between devices  69.7 us (8%)
  other arithmetic  39.4 us (4%)
  between operations  15.3 us (2%)
    all_to_all x4, waiting for transfers between devices, exchange(): return lax.all_to_all(rows, BOTH, split_axis=0, concat_axis=0, tiled=True)  410 us
    dot_general x29, matrix products, mm(): return jnp.einsum(spec, a, b, preferred_element_type=F32)  121 us
    all_to_all x2, waiting for transfers between devices, sum_to_owners(): parts = lax.all_to_all(parts, BOTH, split_axis=0, concat_axis=0, tiled=True)  67.2 us
    all_gather x1, waiting for transfers between devices, per_device(): full = lax.all_gather(packed, BOTH, axis=0, tiled=True)  49.8 us
    all_to_all x3, waiting for transfers between devices, weight_to_expert(): lax.all_to_all(weight, 'fsdp', split_axis=0, concat_axis=1, axis_index_gr...  36.6 us
    unnamed x106, local copies, waits for them, and re-layouts  35.7 us
    all_to_all x3, waiting for transfers between devices, grad_to_owners(): lax.all_to_all(grad.astype(BF16)[None], 'fsdp', split_axis=1, concat_axis...  30.2 us
    unnamed x4, other arithmetic  23.9 us
  transfers between devices with their start and end apart: 13, of which 12 were waited for; matrix products, arithmetic and copies ran while one was open for 21% of the time, Pallas kernels for 0%

profile of v2, /device:TPU:0, one launch (start us, length us, event | category | flops | bytes accessed | tf_op | source)
XLA Modules:
  0.0 914.2 jit_solution(18132010783329984123)
XLA Ops:
  10.5 7.4 all-to-all-start.1
  19.5 25.6 %all-to-all-done.1 = bf16[16,64,512]{2,1,0:T(8,128)(2,1)S(1)} async-done(((bf16[16,64,512]{2,1,0:T(8,128)(2,1)}), bf16[16,64,512]{2,1,0:T(8,128)(2,1)S(1)}, u32[]{:S(2)}, u32[]{:S(2)}) %all-to-all-start.1) | async-done | bytes 1048608 | tf_op jit(solution)/shard_map/all_to_all | solution.py:91
  45.1 6.8 all-to-all-start.2
  52.9 49.8 %all-gather.2.cloned.1.call-done = bf16[1024,3200]{1,0:T(8,128)(2,1)} async-done(((bf16[32,3200]{1,0:T(8,128)(2,1)}), bf16[1024,3200]{1,0:T(8,128)(2,1)}) %all-gather.2.cloned.1.call-update) | async-done | bytes 6553616 | tf_op jit(solution)/shard_map/all_gather | solution.py:166
  126.8 11.0 %all-to-all-done.3 = bf16[16,32,1024]{2,1,0:T(8,128)(2,1)} async-done(((bf16[16,32,1024]{2,1,0:T(8,128)(2,1)}), bf16[16,32,1024]{2,1,0:T(8,128)(2,1)}, u32[]{:S(2)}, u32[]{:S(2)}) %all-to-all-start.3) | async-done | bytes 1048608 | tf_op jit(solution)/shard_map/all_to_all | solution.py:91
  149.6 110.8 %all-to-all-done = bf16[32,80,1024]{2,1,0:T(8,128)(2,1)} async-done(((bf16[32,80,1024]{2,1,0:T(8,128)(2,1)}), bf16[32,80,1024]{2,1,0:T(8,128)(2,1)}, u32[]{:S(2)}, u32[]{:S(2)}) %all-to-all-start) | async-done | bytes 5242912 | tf_op jit(solution)/shard_map/all_to_all | solution.py:116
  265.5 8.1 fusion.120
  273.6 7.1 fusion.119
  280.7 100.8 %all-to-all-done.5 = bf16[32,80,1024]{2,1,0:T(8,128)(2,1)} async-done(((bf16[32,80,1024]{2,1,0:T(8,128)(2,1)}), bf16[32,80,1024]{2,1,0:T(8,128)(2,1)}, u32[]{:S(2)}, u32[]{:S(2)}) %all-to-all-start.5) | async-done | bytes 5242912 | tf_op jit(solution)/shard_map/all_to_all | solution.py:116
  381.6 12.0 %multiply_convert_fusion.1 = (bf16[2560,512]{1,0:T(8,128)(2,1)}, bf16[2560,512]{1,0:T(8,128)(2,1)S(1)}, bf16[2560,512]{1,0:T(8,128)(2,1)}) fusion(f32[2560,512]{1,0:T(8,128)} %fusion.119, f32[2560,512]{1,0:T(8,128)} %fusion.120, bf16[2560,1024]{1,0:T(8,128)(2,1)} %bitcast.37, bf16[512,1024]{1,0:T(8,128)(2,1)} %bitcast.26), kind=kOutput, calls=%fused_computation.6 | convolution fusion | flops 2704015360 | bytes 24641536 | tf_op jit(solution)/shard_map/sd,hd->sh/dot_general | solution.py:31
  402.0 8.0 reduce.10
  425.4 8.0 reduce.11
  440.5 7.0 all-to-all-start.10
  447.5 7.2 convolution_convert_fusion.1
  454.7 15.6 %all-to-all-done.10 = bf16[16,2,16384]{2,1,0:T(2,128)(2,1)S(1)} async-done(((bf16[16,2,16384]{2,1,0:T(2,128)(2,1)}), bf16[16,2,16384]{2,1,0:T(2,128)(2,1)S(1)}, u32[]{:S(2)}, u32[]{:S(2)}) %all-to-all-start.10) | async-done | bytes 1048608 | tf_op jit(solution)/shard_map/all_to_all | solution.py:104
  471.3 6.9 all-to-all-start.4
  489.3 105.1 %all-to-all-done.4 = bf16[32,80,1024]{2,1,0:T(8,128)(2,1)} async-done(((bf16[32,80,1024]{2,1,0:T(8,128)(2,1)}), bf16[32,80,1024]{2,1,0:T(8,128)(2,1)}, u32[]{:S(2)}, u32[]{:S(2)}) %all-to-all-start.4) | async-done | bytes 5242912 | tf_op jit(solution)/shard_map/all_to_all | solution.py:116
  607.9 7.8 reduce.12
  622.7 93.0 %all-to-all-done.6 = bf16[32,80,1024]{2,1,0:T(8,128)(2,1)} async-done(((bf16[32,80,1024]{2,1,0:T(8,128)(2,1)}), bf16[32,80,1024]{2,1,0:T(8,128)(2,1)}, u32[]{:S(2)}, u32[]{:S(2)}) %all-to-all-start.6) | async-done | bytes 5242912 | tf_op jit(solution)/shard_map/all_to_all | solution.py:116
  733.0 10.2 %all-to-all-done.11 = bf16[16,2,16384]{2,1,0:T(2,128)(2,1)S(1)} async-done(((bf16[16,2,16384]{2,1,0:T(2,128)(2,1)}), bf16[16,2,16384]{2,1,0:T(2,128)(2,1)S(1)}, u32[]{:S(2)}, u32[]{:S(2)}) %all-to-all-start.11) | async-done | bytes 1048608 | tf_op jit(solution)/shard_map/all_to_all | solution.py:104
  743.2 6.9 all-to-all-start.8
  783.3 7.7 concatenate.57
  791.0 7.7 all-to-all-done.8
  842.5 59.5 %all-to-all-done.7 = bf16[32,32,2176]{2,1,0:T(8,128)(2,1)} async-done(((bf16[32,32,2176]{2,1,0:T(8,128)(2,1)}), bf16[32,32,2176]{2,1,0:T(8,128)(2,1)}, u32[]{:S(2)}, u32[]{:S(2)}) %all-to-all-start.7) | async-done | bytes 4456480 | tf_op jit(solution)/shard_map/all_to_all | solution.py:129
  (228 shorter events, 208.7 us)
Async XLA Ops:
  7.2 10.8 %copy-start.41 = (s32[1,2,4]{2,1,0:T(2,128)S(1)}, s32[1,2,4]{2,1,0:T(2,128)}, u32[]{:S(2)}) copy-start(s32[1,2,4]{2,1,0:T(2,128)} %param.25) | copy-start | bytes 100
  7.2 11.2 %copy-start.40 = (s32[256,8]{0,1:T(8,128)S(1)}, s32[256,8]{0,1:T(8,128)}, u32[]{:S(2)}) copy-start(s32[256,8]{0,1:T(8,128)} %param.26) | copy-start | bytes 24580
  7.2 12.1 %copy-start.11 = (bf16[256,1024]{1,0:T(8,128)(2,1)S(1)}, bf16[256,1024]{1,0:T(8,128)(2,1)}, u32[]{:S(2)}) copy-start(bf16[256,1024]{1,0:T(8,128)(2,1)} %param.14) | copy-start | bytes 1572868
  7.2 95.5 %all-gather.2.cloned.1.call-start = ((), (), s32[]{:S(2)}) async-start(), calls=%async_computation.12 | async-start | bytes 6758400 | tf_op jit(solution)/shard_map/all_gather | solution.py:166
  10.5 34.6 %all-to-all-start.1 = ((bf16[16,64,512]{2,1,0:T(8,128)(2,1)}), bf16[16,64,512]{2,1,0:T(8,128)(2,1)S(1)}, u32[]{:S(2)}, u32[]{:S(2)}) async-start(bf16[16,64,512]{2,1,0:T(8,128)(2,1)} %param.22), calls=%async_computation.1 | async-start | bytes 2097152 | tf_op jit(solution)/shard_map/all_to_all | solution.py:91
  45.1 62.6 %copy-start.17 = (bf16[16,64,512]{2,1,0:T(8,128)(2,1)}, bf16[16,64,512]{2,1,0:T(8,128)(2,1)S(1)}, u32[]{:S(2)}) copy-start(bf16[16,64,512]{2,1,0:T(8,128)(2,1)S(1)} %all-to-all-done.1) | copy-start | bytes 3145732
  45.1 65.4 %all-to-all-start.2 = ((bf16[16,64,512]{2,1,0:T(8,128)(2,1)}), bf16[16,64,512]{2,1,0:T(8,128)(2,1)}, u32[]{:S(2)}, u32[]{:S(2)}) async-start(bf16[16,64,512]{2,1,0:T(8,128)(2,1)} %param.23), calls=%async_computation.2 | async-start | bytes 2097152 | tf_op jit(solution)/shard_map/all_to_all | solution.py:91
  52.0 55.7 %copy-start.42 = (f32[256]{0:T(256)}, f32[256]{0:T(256)S(1)}, u32[]{:S(2)}) copy-start(f32[256]{0:T(256)S(1)} %add_rsqrt_fusion.1) | copy-start | bytes 3076
  104.2 18.6 %copy-start.31 = (f32[1024]{0:T(1024)}, f32[1024]{0:T(1024)S(1)}, u32[]{:S(2)}) copy-start(f32[1024]{0:T(1024)S(1)} %get-tuple-element.12) | copy-start | bytes 12292
  110.5 27.3 %all-to-all-start.3 = ((bf16[16,32,1024]{2,1,0:T(8,128)(2,1)}), bf16[16,32,1024]{2,1,0:T(8,128)(2,1)}, u32[]{:S(2)}, u32[]{:S(2)}) async-start(bf16[16,32,1024]{2,1,0:T(8,128)(2,1)} %param.24), calls=%async_computation.3 | async-start | bytes 2097152 | tf_op jit(solution)/shard_map/all_to_all | solution.py:91
  122.9 21.3 %copy-start = (bf16[256,1024]{1,0:T(8,128)(2,1)}, bf16[256,1024]{1,0:T(8,128)(2,1)S(1)}, u32[]{:S(2)}) copy-start(bf16[256,1024]{1,0:T(8,128)(2,1)S(1)} %multiply_convert_fusion.4) | copy-start | bytes 1572868
  137.8 8.6 copy-start.24
  137.8 122.6 %all-to-all-start = ((bf16[32,80,1024]{2,1,0:T(8,128)(2,1)}), bf16[32,80,1024]{2,1,0:T(8,128)(2,1)}, u32[]{:S(2)}, u32[]{:S(2)}) async-start(bf16[32,80,1024]{2,1,0:T(8,128)(2,1)} %bitcast.235), calls=%async_computation | async-start | bytes 10485760 | tf_op jit(solution)/shard_map/all_to_all | solution.py:116
  260.4 121.2 %all-to-all-start.5 = ((bf16[32,80,1024]{2,1,0:T(8,128)(2,1)}), bf16[32,80,1024]{2,1,0:T(8,128)(2,1)}, u32[]{:S(2)}, u32[]{:S(2)}) async-start(bf16[32,80,1024]{2,1,0:T(8,128)(2,1)} %multiply_convert_fusion), calls=%async_computation.5 | async-start | bytes 10485760 | tf_op jit(solution)/shard_map/all_to_all | solution.py:116
  265.5 8.1 copy-start.18
  412.7 27.8 %all-to-all-start.9 = ((bf16[16,2,16384]{2,1,0:T(2,128)(2,1)}), bf16[16,2,16384]{2,1,0:T(2,128)(2,1)}, u32[]{:S(2)}, u32[]{:S(2)}) async-start(bf16[16,2,16384]{2,1,0:T(2,128)(2,1)} %reshape.483), calls=%async_computation.9 | async-start | bytes 2097152 | tf_op jit(solution)/shard_map/all_to_all | solution.py:104
  440.5 29.9 %all-to-all-start.10 = ((bf16[16,2,16384]{2,1,0:T(2,128)(2,1)}), bf16[16,2,16384]{2,1,0:T(2,128)(2,1)S(1)}, u32[]{:S(2)}, u32[]{:S(2)}) async-start(bf16[16,2,16384]{2,1,0:T(2,128)(2,1)} %reshape.485), calls=%async_computation.10 | async-start | bytes 2097152 | tf_op jit(solution)/shard_map/all_to_all | solution.py:104
  471.3 123.0 %all-to-all-start.4 = ((bf16[32,80,1024]{2,1,0:T(8,128)(2,1)}), bf16[32,80,1024]{2,1,0:T(8,128)(2,1)}, u32[]{:S(2)}, u32[]{:S(2)}) async-start(bf16[32,80,1024]{2,1,0:T(8,128)(2,1)} %bitcast.245), calls=%async_computation.4 | async-start | bytes 10485760 | tf_op jit(solution)/shard_map/all_to_all | solution.py:116
  594.4 121.3 %all-to-all-start.6 = ((bf16[32,80,1024]{2,1,0:T(8,128)(2,1)}), bf16[32,80,1024]{2,1,0:T(8,128)(2,1)}, u32[]{:S(2)}, u32[]{:S(2)}) async-start(bf16[32,80,1024]{2,1,0:T(8,128)(2,1)} %bitcast.244), calls=%async_computation.6 | async-start | bytes 10485760 | tf_op jit(solution)/shard_map/all_to_all | solution.py:116
  715.6 27.5 %all-to-all-start.11 = ((bf16[16,2,16384]{2,1,0:T(2,128)(2,1)}), bf16[16,2,16384]{2,1,0:T(2,128)(2,1)S(1)}, u32[]{:S(2)}, u32[]{:S(2)}) async-start(bf16[16,2,16384]{2,1,0:T(2,128)(2,1)} %reshape.487), calls=%async_computation.11 | async-start | bytes 2097152 | tf_op jit(solution)/shard_map/all_to_all | solution.py:104
  743.2 10.1 %copy-start.4 = (bf16[16,2,16384]{2,1,0:T(2,128)(2,1)}, bf16[16,2,16384]{2,1,0:T(2,128)(2,1)S(1)}, u32[]{:S(2)}) copy-start(bf16[16,2,16384]{2,1,0:T(2,128)(2,1)S(1)} %all-to-all-done.11) | copy-start | bytes 3145732
  743.2 55.6 %all-to-all-start.8 = ((bf16[32,32,1024]{2,1,0:T(8,128)(2,1)}), bf16[32,32,1024]{2,1,0:T(8,128)(2,1)}, u32[]{:S(2)}, u32[]{:S(2)}) async-start(bf16[32,32,1024]{2,1,0:T(8,128)(2,1)} %bitcast.237), calls=%async_computation.8 | async-start | bytes 4194304 | tf_op jit(solution)/shard_map/all_to_all | solution.py:129
  750.1 9.1 copy-start.34
  798.7 103.3 %all-to-all-start.7 = ((bf16[32,32,2176]{2,1,0:T(8,128)(2,1)}), bf16[32,32,2176]{2,1,0:T(8,128)(2,1)}, u32[]{:S(2)}, u32[]{:S(2)}) async-start(bf16[32,32,2176]{2,1,0:T(8,128)(2,1)} %bitcast.236), calls=%async_computation.7 | async-start | bytes 8912896 | tf_op jit(solution)/shard_map/all_to_all | solution.py:129
  (36 other events, 117.9 us)
Sparse Core Ops, SparseCore 0:
  11.5 91.1 all-gather.1
